TPU v7x, 32 devices: a whole 2x2x4 slice. The times are simulated.
32 devices in a mesh: st: 8 (over z, x), gr: 4 (over y, core).
Axes of the slice: x: 2, y: 2, z: 4, core: 2. Of those that a mesh axis runs over, the one named last changes fastest.
Arguments:
- states: float32 [32, 24, 768], P(('st', 'gr')), may hold values from -6 to 6
- regions: int32 [24, 768], replicated, may hold values from 0 to 7
- pot_table: float32 [8], replicated, may hold values from -3 to 0
- subspace: bfloat16 [32, 32], P(None, 'st'), may hold values from -1.5 to 1.5
- state_order: int32 [32], replicated, may hold values from 0 to 31, each once
Outputs:
- rotated: bfloat16 [32, 24, 768], P('st', 'gr')
Inputs may be any that keep to these rules, and one draw needn't show every extreme that they name: state_order is a permutation of the window positions.
All inputs are finite; a program needn't handle non-finite values.
Results may differ from a plain program's by a relative error of at most 0.0049.
Values may be sent and summed in bfloat16 or wider, within the bound.
No kernel may reach another device: no remote copies, remote signals or barrier semaphores. Data moves between devices by JAX's collectives and lax.ppermute only.
A program may use at most 64 MiB of HBM per device.

v0:
```python
import jax
import jax.numpy as jnp
from jax import lax
from jax.sharding import PartitionSpec as P

NY = 24
NZ = 32
DEG = 4


coef_center = -5369.0 / 1800.0
coef_list = (12.0 / 7.0, -15.0 / 56.0, 10.0 / 189.0, -1.0 / 112.0, 2.0 / 1925.0, -1.0 / 16632.0)
centre = 6.75
half_width = 5.25


def shift_cols(field, offset):
    width = field.shape[1]
    if offset > 0:
        return jnp.pad(field[:, offset:], ((0, 0), (0, offset)))
    return jnp.pad(field[:, : width + offset], ((0, 0), (-offset, 0)))


def shift_rows(field, offset):
    height = field.shape[0]
    if offset > 0:
        return jnp.pad(field[offset:, :], ((0, offset), (0, 0)))
    return jnp.pad(field[: height + offset, :], ((-offset, 0), (0, 0)))


def laplace(field):
    zpos = lax.broadcasted_iota(jnp.int32, field.shape, 1) % NZ
    total = 3.0 * coef_center * field
    for step in range(1, 7):
        xpair = shift_rows(field, step) + shift_rows(field, -step)
        ypair = shift_cols(field, step * NZ) + shift_cols(field, -step * NZ)
        zplus = jnp.where(zpos + step < NZ, shift_cols(field, step), 0.0)
        zminus = jnp.where(zpos - step >= 0, shift_cols(field, -step), 0.0)
        total = total + coef_list[step - 1] * (xpair + ypair + (zplus + zminus))
    return total


def shifted_op(field, potential):
    return -0.5 * laplace(field) + potential * field - centre * field


def lookup(regions, pot_table):
    levels = lax.broadcasted_iota(jnp.int32, (pot_table.shape[0], 1, 1), 0)
    hits = regions[None, :, :] == levels
    return jnp.sum(jnp.where(hits, pot_table[:, None, None], 0.0), axis=0)


def per_device(states, regions, pot_table, subspace, state_order):
    potential = lookup(regions, pot_table)
    previous = states[0]
    current = shifted_op(previous, potential) * (1.0 / half_width)
    for step in range(1, DEG):
        following = shifted_op(current, potential) * (2.0 / half_width) - previous
        previous = current
        current = following
    filtered = current.astype(jnp.bfloat16)
    groups = lax.axis_size("gr")
    weights = jnp.take(subspace, state_order, axis=0)
    columns = weights.shape[1]
    blocks = lax.all_to_all(filtered[None], "gr", split_axis=1, concat_axis=0, tiled=True)
    slab_rows = blocks.shape[1]
    flat_blocks = blocks.reshape(groups, slab_rows * NY * NZ)
    summed = lax.dot_general(
        weights,
        lax.all_gather(flat_blocks, "st", axis=0, tiled=True),
        (((0,), (0,)), ((), ())),
        preferred_element_type=jnp.float32,
    )
    return summed.reshape(columns, slab_rows, NY * NZ).astype(jnp.bfloat16)


def solution(mesh):
    in_specs = (P(("st", "gr"), None, None), P(), P(), P(None, "st"), P())
    out_specs = P("st", "gr", None)
    return jax.shard_map(
        per_device, mesh=mesh, in_specs=in_specs, out_specs=out_specs, check_vma=False
    )
```

profile of v0, /device:TPU:0, one launch (start us, length us, event | category | flops | bytes accessed | tf_op | source)
XLA Modules:
  0.0 51.4 jit_solution(2509546299188329413)
XLA Ops:
  0.0 1.1 %fusion.75 = (f32[24,736]{1,0:T(8,128)S(1)}, f32[24,736]{1,0:T(8,128)S(1)}) fusion(f32[24,768]{1,0:T(8,128)} %bitcast.37), kind=kLoop, calls=%fused_computation.112 | loop fusion | bytes 282624 | tf_op jit(solution)/shard_map/slice | solution.py:20
  1.1 0.1 fusion.76
  1.2 0.1 fusion.77
  1.3 0.1 fusion.78
  1.3 0.1 fusion.79
  1.4 0.1 fusion.80
  1.5 0.1 fusion.82
  1.6 0.1 fusion.84
  1.7 0.1 fusion.86
  1.8 0.1 fusion.83
  1.9 0.1 fusion.85
  2.1 0.0 copy-start.1
  2.1 0.8 %copy-done.1 = s32[24,768]{1,0:T(8,128)S(1)} copy-done((s32[24,768]{1,0:T(8,128)S(1)}, s32[24,768]{1,0:T(8,128)}, u32[]{:S(2)}) %copy-start.1) | copy-done | bytes 73752
  3.0 0.1 select_reduce_fusion
  3.1 0.4 broadcast_multiply_fusion
  3.5 0.1 fusion.68
  3.7 0.1 fusion.71
  3.8 0.1 fusion.74
  3.9 0.1 fusion.58
  3.9 0.1 fusion.59
  4.1 0.1 fusion.61
  4.1 0.1 fusion.62
  4.3 0.1 fusion.64
  4.3 0.1 fusion.65
  4.5 0.1 fusion.70
  4.5 0.1 fusion.73
  4.6 0.4 multiply_subtract_fusion.1
  5.1 0.1 fusion.40
  5.2 0.1 fusion.41
  5.3 0.1 fusion.43
  5.4 0.1 fusion.44
  5.5 0.1 fusion.46
  5.5 0.1 fusion.47
  5.7 0.1 fusion.50
  5.8 0.1 fusion.53
  5.9 0.1 fusion.56
  6.0 0.1 fusion.52
  6.1 0.1 fusion.55
  6.1 0.4 multiply_subtract_fusion
  6.6 0.1 fusion.22
  6.7 0.1 fusion.23
  6.8 0.1 fusion.25
  6.9 0.1 fusion.26
  7.0 0.1 fusion.28
  7.0 0.1 fusion.29
  7.2 0.1 fusion.32
  7.3 0.1 fusion.35
  7.4 0.1 fusion.38
  7.5 0.1 fusion.34
  7.6 0.1 fusion.37
  7.7 0.4 fusion.12
  8.1 0.1 copy.19
  8.2 0.5 broadcast.651
  8.7 0.8 %reduce.2 = bf16[24,768]{1,0:T(8,128)(2,1)S(1)} reduce(bf16[24,1,768]{2,1,0:T(2,128)(2,1)S(1)} %bitcast.49, bf16[]{:T(256)} %broadcast.651), dimensions={1}, to_apply=%bitcast.36.reduce_sub_computation | reduce | bytes 73730
  9.5 0.6 %reshape.42 = bf16[4,2,2304]{2,1,0:T(2,128)(2,1)} reshape(bf16[24,768]{1,0:T(8,128)(2,1)S(1)} %reduce.2) | data formatting | bytes 73728
  10.2 4.4 %all-to-all-start = ((bf16[4,2,2304]{2,1,0:T(2,128)(2,1)}), bf16[4,2,2304]{2,1,0:T(2,128)(2,1)S(1)}, u32[]{:S(2)}, u32[]{:S(2)}) async-start(bf16[4,2,2304]{2,1,0:T(2,128)(2,1)} %reshape.42), calls=%async_computation | async-start | bytes 73728 | tf_op jit(solution)/shard_map/all_to_all | solution.py:65
  14.6 0.7 %copy-done.2 = bf16[32,4]{0,1:T(4,128)(2,1)S(1)} copy-done((bf16[32,4]{0,1:T(4,128)(2,1)S(1)}, bf16[32,4]{0,1:T(4,128)(2,1)}, u32[]{:S(2)}) %copy-start.2) | copy-done | bytes 280
  15.3 0.1 copy.15
  15.4 0.6 %gather_fusion = bf16[32,4]{1,0:T(8,128)(2,1)S(1)} fusion(bf16[32,4]{1,0:T(8,128)(2,1)S(1)} %copy.15, s32[1024]{0:T(1024)S(1)} %pad_clamp_fusion), kind=kCustom, calls=%fused_computation | custom fusion | bytes 640 | tf_op jit(solution)/shard_map/jit(_take)/gather | solution.py:63
  16.0 2.6 %all-to-all-done = bf16[4,2,2304]{2,1,0:T(2,128)(2,1)S(1)} async-done(((bf16[4,2,2304]{2,1,0:T(2,128)(2,1)}), bf16[4,2,2304]{2,1,0:T(2,128)(2,1)S(1)}, u32[]{:S(2)}, u32[]{:S(2)}) %all-to-all-start) | async-done | bytes 36896 | tf_op jit(solution)/shard_map/all_to_all | solution.py:65
  18.6 0.2 bitcast_reduce_fusion
  18.8 31.6 %all-gather = bf16[8,4,4608]{2,1,0:T(4,128)(2,1)S(1)} all-gather(bf16[1,4,4608]{2,1,0:T(4,128)(2,1)S(1)} %reshape.38), channel_id=1, replica_groups=mesh['st'=8,'gr'=4] {'st'}, dimensions={0}, use_global_device_ids=true | all-gather | bytes 331776 | tf_op jit(solution)/shard_map/all_gather | solution.py:70
  50.4 0.1 reshape.39
  50.5 0.9 %convolution_convert_fusion = bf16[4,4608]{1,0:T(4,128)(2,1)} fusion(bf16[32,4608]{1,0:T(8,128)(2,1)S(1)} %reshape.39, bf16[32,4]{1,0:T(8,128)(2,1)S(1)} %gather_fusion, pred[32]{0:T(512)(128)(4,1)S(1)} %compare_and_fusion), kind=kOutput, calls=%fused_computation.1 | convolution fusion | flops 1198208 | bytes 332064 | tf_op jit(solution)/shard_map/dot_general | solution.py:68
  (42 shorter events, 0.5 us)
Async XLA Ops:
  0.0 1.1 %copy-start = (f32[1,24,768]{2,1,0:T(8,128)S(1)}, f32[1,24,768]{2,1,0:T(8,128)}, u32[]{:S(2)}) copy-start(f32[1,24,768]{2,1,0:T(8,128)} %param.5) | copy-start | bytes 221188
  2.1 0.9 %copy-start.1 = (s32[24,768]{1,0:T(8,128)S(1)}, s32[24,768]{1,0:T(8,128)}, u32[]{:S(2)}) copy-start(s32[24,768]{1,0:T(8,128)} %param.6) | copy-start | bytes 221188
  2.1 0.9 %copy-start.3 = (f32[8]{0:T(128)S(1)}, f32[8]{0:T(128)}, u32[]{:S(2)}) copy-start(f32[8]{0:T(128)} %param.7) | copy-start | bytes 100
  10.2 4.4 %copy-start.4 = (s32[32]{0:T(128)S(1)}, s32[32]{0:T(128)}, u32[]{:S(2)}) copy-start(s32[32]{0:T(128)} %param.9) | copy-start | bytes 388
  10.2 8.4 %all-to-all-start = ((bf16[4,2,2304]{2,1,0:T(2,128)(2,1)}), bf16[4,2,2304]{2,1,0:T(2,128)(2,1)S(1)}, u32[]{:S(2)}, u32[]{:S(2)}) async-start(bf16[4,2,2304]{2,1,0:T(2,128)(2,1)} %reshape.42), calls=%async_computation | async-start | bytes 73728 | tf_op jit(solution)/shard_map/all_to_all | solution.py:65
  14.6 0.7 %copy-start.2 = (bf16[32,4]{0,1:T(4,128)(2,1)S(1)}, bf16[32,4]{0,1:T(4,128)(2,1)}, u32[]{:S(2)}) copy-start(bf16[32,4]{0,1:T(4,128)(2,1)} %param.8) | copy-start | bytes 772
where the time goes:
time: 51.7 us; the launch traced here: 51.4 us
  blocking collectives  31.6 us (61%)
  local copies, waits for them, and re-layouts  8.8 us (17%)
  starting transfers between devices  4.4 us (9%)
  other arithmetic  2.71 us (5%)
  waiting for transfers between devices  2.57 us (5%)
  matrix products  0.91 us (2%)
    all_gather x1, blocking collectives, per_device(): lax.all_gather(flat_blocks, 'st', axis=0, tiled=True)  31.6 us
    slice x48, local copies, waits for them, and re-layouts, shift_cols(): return jnp.pad(field[:, offset:], ((0, 0), (0, offset)))  4.65 us
    all_to_all x1, starting transfers between devices, per_device(): lax.all_to_all(filtered[None], 'gr', split_axis=1, concat_axis=0, tiled=T...  4.4 us
    unnamed x16, local copies, waits for them, and re-layouts  2.9 us
    all_to_all x1, waiting for transfers between devices, per_device(): lax.all_to_all(filtered[None], 'gr', split_axis=1, concat_axis=0, tiled=T...  2.57 us
  transfers between devices with their start and end apart: 1, of which 1 were waited for; matrix products, arithmetic and copies ran while one was open for 1% of the time, Pallas kernels for 0%

commit v1 on v0

v1 whole, which is shorter than its diff:
```python
import functools

import jax
import jax.numpy as jnp
from jax import lax
from jax.experimental import pallas as pl
from jax.experimental.pallas import tpu as pltpu
from jax.sharding import PartitionSpec as P

NZ = 32
DEG = 4
LANES = 128

coef_center = -5369.0 / 1800.0
coef_list = (12.0 / 7.0, -15.0 / 56.0, 10.0 / 189.0, -1.0 / 112.0, 2.0 / 1925.0, -1.0 / 16632.0)
centre = 6.75
half_width = 5.25


def roll(value, shift, axis):
    size = value.shape[axis]
    shift = shift % size
    return value if shift == 0 else pltpu.roll(value, shift, axis)


def scaled_op(tiles, diagonal, zmasks, lane, row):
    count = len(tiles)
    height = tiles[0].shape[0]
    per_tile = LANES // NZ
    zero = jnp.zeros_like(tiles[0])
    turned = [[roll(t, NZ * k, 1) for k in range(per_tile)] for t in tiles]

    def at(k, t):
        return turned[t][k] if 0 <= t < count else zero

    result = []
    for t, tile in enumerate(tiles):
        total = diagonal[t] * tile
        for step in range(1, len(coef_list) + 1):
            weight = -0.5 * coef_list[step - 1] / half_width
            up = jnp.where(row < height - step, roll(tile, -step, 0), 0.0)
            down = jnp.where(row >= step, roll(tile, step, 0), 0.0)
            whole, part = divmod(step, per_tile)
            if part == 0:
                right, left = at(0, t + whole), at(0, t - whole)
            else:
                edge = LANES - NZ * part
                other = per_tile - part
                right = jnp.where(lane < edge, at(other, t + whole), at(other, t + whole + 1))
                left = jnp.where(lane >= NZ * part, at(part, t - whole), at(part, t - whole - 1))
            total = total + weight * ((up + down) + (right + left))
            plus, minus = zmasks[step - 1]
            total = total + (plus * roll(tile, -step, 1) + minus * roll(tile, step, 1))
        result.append(total)
    return result


def filter_kernel(table_ref, state_ref, regions_ref, out_ref):
    height, width = regions_ref.shape
    count = width // LANES
    levels = table_ref.shape[0]
    copies, groups = out_ref.shape[0], out_ref.shape[1]
    slab = height // groups
    shape = (height, LANES)
    lane = lax.broadcasted_iota(jnp.int32, shape, 1)
    row = lax.broadcasted_iota(jnp.int32, shape, 0)
    zpos = lane % NZ
    zmasks = []
    for step in range(1, len(coef_list) + 1):
        weight = -0.5 * coef_list[step - 1] / half_width
        zmasks.append(
            (jnp.where(zpos + step < NZ, weight, 0.0), jnp.where(zpos - step >= 0, weight, 0.0))
        )
    diagonal, previous = [], []
    for t in range(count):
        window = slice(t * LANES, (t + 1) * LANES)
        region = regions_ref[:, window]
        potential = jnp.zeros(shape, jnp.float32)
        for level in range(levels):
            potential = jnp.where(region == level, table_ref[level], potential)
        diagonal.append((potential - (centre + 1.5 * coef_center)) * (1.0 / half_width))
        previous.append(state_ref[0, :, window])
    current = scaled_op(previous, diagonal, zmasks, lane, row)
    for _ in range(1, DEG):
        applied = scaled_op(current, diagonal, zmasks, lane, row)
        following = [2.0 * a - p for a, p in zip(applied, previous)]
        previous, current = current, following
    for g in range(groups):
        for t in range(count):
            piece = current[t][g * slab : (g + 1) * slab].astype(jnp.bfloat16)
            for c in range(copies):
                out_ref[c, g, t * slab : (t + 1) * slab, :] = piece


def rotate_kernel(order_ref, weights_ref, blocks_ref, out_ref):
    states = blocks_ref.shape[0]
    slab, columns, width = out_ref.shape
    shape = blocks_ref.shape[1:]

    def body(s, totals):
        block = blocks_ref[s].astype(jnp.float32)
        base = order_ref[s] * columns
        return tuple(total + weights_ref[base + j] * block for j, total in enumerate(totals))

    unroll = 8 if states % 8 == 0 else 1
    totals = lax.fori_loop(
        0, states, body, tuple(jnp.zeros(shape, jnp.float32) for _ in range(columns)), unroll=unroll
    )
    for j in range(columns):
        for t in range(width // LANES):
            out_ref[:, j, t * LANES : (t + 1) * LANES] = totals[j][t * slab : (t + 1) * slab].astype(out_ref.dtype)


def grant(array):
    return 3 * array.size * array.dtype.itemsize + (4 << 20)


def per_device(st, gr, states, regions, pot_table, subspace, state_order):
    height, width = regions.shape
    slab = height // gr
    rows = slab * width // LANES
    columns = subspace.shape[1]
    vmem, smem = pl.BlockSpec(memory_space=pltpu.VMEM), pl.BlockSpec(memory_space=pltpu.SMEM)
    filtered = jax.ShapeDtypeStruct((st, gr, rows, LANES), jnp.bfloat16)
    outgoing = pl.pallas_call(
        filter_kernel,
        out_shape=filtered,
        in_specs=[smem, vmem, vmem],
        out_specs=vmem,
    )(pot_table, states, regions)
    blocks = lax.all_to_all(
        outgoing.reshape(st * gr, rows, LANES), ("st", "gr"), split_axis=0, concat_axis=0, tiled=True
    )
    weights = subspace.astype(jnp.float32).reshape(-1)
    rotated = pl.pallas_call(
        rotate_kernel,
        out_shape=jax.ShapeDtypeStruct((slab, columns, width), jnp.bfloat16),
        in_specs=[smem, smem, vmem],
        out_specs=vmem,
        compiler_params=pltpu.CompilerParams(vmem_limit_bytes=grant(blocks)),
    )(state_order, weights, blocks)
    return rotated.transpose(1, 0, 2)


def solution(mesh):
    in_specs = (P(("st", "gr"), None, None), P(), P(), P(None, "st"), P())
    out_specs = P("st", "gr", None)
    body = functools.partial(per_device, mesh.shape["st"], mesh.shape["gr"])
    return jax.shard_map(body, mesh=mesh, in_specs=in_specs, out_specs=out_specs, check_vma=False)
```

time: 51.7 us -> 24.2 us (0.47)
  blocking collectives: 31.6 us -> 0 us
  waiting for transfers between devices: 2.57 us -> 11.8 us
  local copies, waits for them, and re-layouts: 8.8 us -> 0.2 us
  Pallas kernels: 0 us -> 4.55 us
  starting transfers between devices: 4.4 us -> 7.33 us
  other arithmetic: 2.71 us -> 0 us
  matrix products: 0.91 us -> 0 us
    all_gather x1 -> x0, blocking collectives: 31.6 us -> none  [per_device(): lax.all_gather(flat_blocks, 'st', axis=0, tiled=True)]
    all_to_all x1, waiting for transfers between devices: 2.57 us -> 11.8 us  [per_device(): lax.all_to_all(outgoing.reshape(st * gr, rows, LANES), ('st', 'gr'), spli...]
    slice x72 -> x0, local copies, waits for them, and re-layouts: 5.05 us -> none  [the longest x48 4.65 us: shift_cols(): return jnp.pad(field[:, offset:], ((0, 0), (0, offset)))]
    pallas_call x0 -> x2, Pallas kernels: none -> 4.55 us  [the longest x1 3.04 us: per_device(): pl.pallas_call(filter_kernel, out_shape=filtered, in_specs=[smem, vmem, v...]
    all_to_all x1, starting transfers between devices: 4.4 us -> 7.33 us  [per_device(): lax.all_to_all(outgoing.reshape(st * gr, rows, LANES), ('st', 'gr'), spli...]
    unnamed x16 -> x4, local copies, waits for them, and re-layouts: 2.9 us -> 0.01 us
    dot_general x1 -> x0, matrix products: 0.91 us -> none  [per_device(): lax.dot_general(weights, lax.all_gather(flat_blocks, 'st', axis=0, tiled=...]
    sub x2 -> x0, other arithmetic: 0.86 us -> none  [per_device(): following = shifted_op(current, potential) * (2.0 / half_width) - previous]
where the time goes in v1:
time: 24.2 us; the launch traced here: 23.9 us
  waiting for transfers between devices  11.8 us (49%)
  starting transfers between devices  7.33 us (30%)
  Pallas kernels  4.55 us (19%)
    all_to_all x1, waiting for transfers between devices, per_device(): lax.all_to_all(outgoing.reshape(st * gr, rows, LANES), ('st', 'gr'), spli...  11.8 us
    all_to_all x1, starting transfers between devices, per_device(): lax.all_to_all(outgoing.reshape(st * gr, rows, LANES), ('st', 'gr'), spli...  7.33 us
    pallas_call x1, Pallas kernels, per_device(): pl.pallas_call(filter_kernel, out_shape=filtered, in_specs=[smem, vmem, v...  3.04 us
    pallas_call x1, Pallas kernels, per_device(): pl.pallas_call(rotate_kernel, out_shape=jax.ShapeDtypeStruct((slab, colum...  1.51 us
  transfers between devices with their start and end apart: 1, of which 1 were waited for; matrix products, arithmetic and copies ran while one was open for 1% of the time, Pallas kernels for 0%

profile of v1, /device:TPU:0, one launch (start us, length us, event | category | flops | bytes accessed | tf_op | source)
XLA Modules:
  0.0 23.9 jit_solution(4014796690591223112)
XLA Ops:
  0.0 3.0 %shard_map.55 = bf16[8,4,36,128]{3,2,1,0:T(8,128)(2,1)} custom-call(f32[8]{0:T(128)} %table_ref.1, f32[1,24,768]{2,1,0:T(8,128)} %state_ref.1, s32[24,768]{1,0:T(8,128)} %regions_ref.1), custom_call_target="tpu_custom_call" | custom-call | tf_op jit(solution)/shard_map/pallas_call | solution.py:125
  3.0 0.0 copy-start.1
  3.0 7.3 %all-to-all-start = ((bf16[32,36,128]{2,1,0:T(8,128)(2,1)}), bf16[32,36,128]{2,1,0:T(8,128)(2,1)S(1)}, u32[]{:S(2)}, u32[]{:S(2)}) async-start(bf16[32,36,128]{2,1,0:T(8,128)(2,1)} %bitcast.2), calls=%async_computation | async-start | bytes 655360 | tf_op jit(solution)/shard_map/all_to_all | solution.py:131
  10.4 0.0 copy-done.1
  10.4 0.1 copy.7
  10.5 0.0 copy-start
  10.5 0.1 reshape.12.weights_ref
  10.6 11.8 %all-to-all-done.blocks_ref = bf16[32,36,128]{2,1,0:T(8,128)(2,1)S(1)} async-done(((bf16[32,36,128]{2,1,0:T(8,128)(2,1)}), bf16[32,36,128]{2,1,0:T(8,128)(2,1)S(1)}, u32[]{:S(2)}, u32[]{:S(2)}) %all-to-all-start) | async-done | bytes 294944 | tf_op jit(solution)/shard_map/all_to_all | solution.py:131
  22.4 0.0 copy-done
  22.4 1.5 %shard_map.56 = bf16[6,4,768]{2,1,0:T(4,128)(2,1)} custom-call(s32[32]{0:T(128)S(1)} %copy-done, f32[128]{0:T(128)S(1)} %reshape.12.weights_ref, bf16[32,36,128]{2,1,0:T(8,128)(2,1)S(1)} %all-to-all-done.blocks_ref), custom_call_target="tpu_custom_call" | custom-call | tf_op jit(solution)/shard_map/pallas_call | solution.py:135
Async XLA Ops:
  3.0 7.3 %copy-start.1 = (bf16[32,4]{0,1:T(4,128)(2,1)S(1)}, bf16[32,4]{0,1:T(4,128)(2,1)}, u32[]{:S(2)}) copy-start(bf16[32,4]{0,1:T(4,128)(2,1)} %param.8) | copy-start | bytes 772
  3.0 19.4 %all-to-all-start = ((bf16[32,36,128]{2,1,0:T(8,128)(2,1)}), bf16[32,36,128]{2,1,0:T(8,128)(2,1)S(1)}, u32[]{:S(2)}, u32[]{:S(2)}) async-start(bf16[32,36,128]{2,1,0:T(8,128)(2,1)} %bitcast.2), calls=%async_computation | async-start | bytes 655360 | tf_op jit(solution)/shard_map/all_to_all | solution.py:131
  10.5 11.9 %copy-start = (s32[32]{0:T(128)S(1)}, s32[32]{0:T(128)}, u32[]{:S(2)}) copy-start(s32[32]{0:T(128)} %order_ref.1) | copy-start | bytes 388

commit v2 on v1

--- a/solution.py
+++ b/solution.py
@@ -55,11 +55,20 @@
     return result
 
 
-def filter_kernel(table_ref, state_ref, regions_ref, out_ref):
+def filter_kernel(
+    state_hbm, regions_hbm, table_hbm, order_hbm, subspace_hbm,
+    out_ref, weights_ref,
+    state_ref, regions_ref, table_ref, order_ref, subspace_ref, sems,
+):
+    sources = (regions_hbm, table_hbm, state_hbm, order_hbm, subspace_hbm)
+    targets = (regions_ref, table_ref, state_ref, order_ref, subspace_ref)
+    copies = [pltpu.make_async_copy(a, b, sems.at[i]) for i, (a, b) in enumerate(zip(sources, targets))]
+    for copy in copies:
+        copy.start()
     height, width = regions_ref.shape
     count = width // LANES
     levels = table_ref.shape[0]
-    copies, groups = out_ref.shape[0], out_ref.shape[1]
+    groups = out_ref.shape[0]
     slab = height // groups
     shape = (height, LANES)
     lane = lax.broadcasted_iota(jnp.int32, shape, 1)
@@ -71,15 +80,17 @@
         zmasks.append(
             (jnp.where(zpos + step < NZ, weight, 0.0), jnp.where(zpos - step >= 0, weight, 0.0))
         )
-    diagonal, previous = [], []
+    diagonal = []
+    copies[0].wait()
+    copies[1].wait()
     for t in range(count):
-        window = slice(t * LANES, (t + 1) * LANES)
-        region = regions_ref[:, window]
+        region = regions_ref[:, t * LANES : (t + 1) * LANES]
         potential = jnp.zeros(shape, jnp.float32)
         for level in range(levels):
             potential = jnp.where(region == level, table_ref[level], potential)
         diagonal.append((potential - (centre + 1.5 * coef_center)) * (1.0 / half_width))
-        previous.append(state_ref[0, :, window])
+    copies[2].wait()
+    previous = [state_ref[0, :, t * LANES : (t + 1) * LANES] for t in range(count)]
     current = scaled_op(previous, diagonal, zmasks, lane, row)
     for _ in range(1, DEG):
         applied = scaled_op(current, diagonal, zmasks, lane, row)
@@ -88,19 +99,28 @@
     for g in range(groups):
         for t in range(count):
             piece = current[t][g * slab : (g + 1) * slab].astype(jnp.bfloat16)
-            for c in range(copies):
-                out_ref[c, g, t * slab : (t + 1) * slab, :] = piece
+            out_ref[g, t * slab : (t + 1) * slab, :] = piece
+    copies[3].wait()
+    copies[4].wait()
+    columns, states = subspace_ref.shape
+    place = lax.broadcasted_iota(jnp.int32, (states, states), 0)
+    here = lax.broadcasted_iota(jnp.int32, (states, states), 1)
+    chosen = jnp.where(order_ref[...] == place, 1.0, 0.0).astype(jnp.bfloat16)
+    weights = jnp.dot(subspace_ref[...], chosen, preferred_element_type=jnp.float32)
+    ones = jnp.ones((states, LANES), jnp.bfloat16)
+    for j in range(columns):
+        spread = jnp.where(place == here, weights[j : j + 1], 0.0).astype(jnp.bfloat16)
+        weights_ref[j] = jnp.dot(spread, ones, preferred_element_type=jnp.float32)
 
 
-def rotate_kernel(order_ref, weights_ref, blocks_ref, out_ref):
+def rotate_kernel(weights_ref, blocks_ref, out_ref):
     states = blocks_ref.shape[0]
     slab, columns, width = out_ref.shape
     shape = blocks_ref.shape[1:]
 
     def body(s, totals):
         block = blocks_ref[s].astype(jnp.float32)
-        base = order_ref[s] * columns
-        return tuple(total + weights_ref[base + j] * block for j, total in enumerate(totals))
+        return tuple(total + weights_ref[j, pl.ds(s, 1)] * block for j, total in enumerate(totals))
 
     unroll = 8 if states % 8 == 0 else 1
     totals = lax.fori_loop(
@@ -120,25 +140,30 @@
     slab = height // gr
     rows = slab * width // LANES
     columns = subspace.shape[1]
-    vmem, smem = pl.BlockSpec(memory_space=pltpu.VMEM), pl.BlockSpec(memory_space=pltpu.SMEM)
-    filtered = jax.ShapeDtypeStruct((st, gr, rows, LANES), jnp.bfloat16)
-    outgoing = pl.pallas_call(
+    hbm = pl.BlockSpec(memory_space=pltpu.HBM)
+    vmem = pl.BlockSpec(memory_space=pltpu.VMEM)
+    filtered = jax.ShapeDtypeStruct((gr, rows, LANES), jnp.bfloat16)
+    order = state_order.reshape(1, -1)
+    inputs = [pltpu.with_memory_space_constraint(a, pltpu.HBM) for a in (states, regions, pot_table, order, subspace.T)]
+    spaces = (pltpu.VMEM, pltpu.VMEM, pltpu.SMEM, pltpu.VMEM, pltpu.VMEM)
+    outgoing, weights = pl.pallas_call(
         filter_kernel,
-        out_shape=filtered,
-        in_specs=[smem, vmem, vmem],
-        out_specs=vmem,
-    )(pot_table, states, regions)
+        out_shape=(filtered, jax.ShapeDtypeStruct((columns, subspace.shape[0], LANES), jnp.float32)),
+        in_specs=[hbm] * 5,
+        out_specs=(vmem, vmem),
+        scratch_shapes=[space(a.shape, a.dtype) for space, a in zip(spaces, inputs)] + [pltpu.SemaphoreType.DMA((5,))],
+        compiler_params=pltpu.CompilerParams(vmem_limit_bytes=grant(filtered)),
+    )(*inputs)
     blocks = lax.all_to_all(
-        outgoing.reshape(st * gr, rows, LANES), ("st", "gr"), split_axis=0, concat_axis=0, tiled=True
+        jnp.broadcast_to(outgoing, (st, gr, rows, LANES)).reshape(st * gr, rows, LANES), ("st", "gr"), split_axis=0, concat_axis=0, tiled=True
     )
-    weights = subspace.astype(jnp.float32).reshape(-1)
     rotated = pl.pallas_call(
         rotate_kernel,
         out_shape=jax.ShapeDtypeStruct((slab, columns, width), jnp.bfloat16),
-        in_specs=[smem, smem, vmem],
+        in_specs=[vmem, vmem],
         out_specs=vmem,
         compiler_params=pltpu.CompilerParams(vmem_limit_bytes=grant(blocks)),
-    )(state_order, weights, blocks)
+    )(weights, blocks)
     return rotated.transpose(1, 0, 2)
 
 

time: 24.2 us -> 22.9 us (0.946)
  blocking collectives: 0 us -> 19.2 us
  waiting for transfers between devices: 11.8 us -> 0 us
  starting transfers between devices: 7.33 us -> 0 us
  Pallas kernels: 4.55 us -> 3.51 us
    all_to_all x0 -> x1, blocking collectives: none -> 19.2 us  [per_device(): lax.all_to_all(jnp.broadcast_to(outgoing, (st, gr, rows, LANES)).reshape(...]
    all_to_all x1 -> x0, waiting for transfers between devices: 11.8 us -> none  [per_device(): lax.all_to_all(outgoing.reshape(st * gr, rows, LANES), ('st', 'gr'), spli...]
    all_to_all x1 -> x0, starting transfers between devices: 7.33 us -> none  [per_device(): lax.all_to_all(outgoing.reshape(st * gr, rows, LANES), ('st', 'gr'), spli...]
    pallas_call x1, Pallas kernels: 1.51 us -> 0.93 us  [per_device(): pl.pallas_call(rotate_kernel, out_shape=jax.ShapeDtypeStruct((slab, colum...]
    pallas_call x1, Pallas kernels: 3.04 us -> 2.57 us  [per_device(): pl.pallas_call(filter_kernel, out_shape=(filtered, jax.ShapeDtypeStruct((...]
  transfers between devices with their start and end apart: 1 -> 0, of which waited for: 1 -> 0; matrix products, arithmetic and copies ran while one was open for 1% -> 0% of each run, Pallas kernels for 0% -> 0%
where the time goes in v2:
time: 22.9 us; the launch traced here: 22.7 us
  blocking collectives  19.2 us (84%)
  Pallas kernels  3.51 us (15%)
    all_to_all x1, blocking collectives, per_device(): lax.all_to_all(jnp.broadcast_to(outgoing, (st, gr, rows, LANES)).reshape(...  19.2 us
    pallas_call x1, Pallas kernels, per_device(): pl.pallas_call(filter_kernel, out_shape=(filtered, jax.ShapeDtypeStruct((...  2.57 us
    pallas_call x1, Pallas kernels, per_device(): pl.pallas_call(rotate_kernel, out_shape=jax.ShapeDtypeStruct((slab, colum...  0.93 us

profile of v2, /device:TPU:0, one launch (start us, length us, event | category | flops | bytes accessed | tf_op | source)
XLA Modules:
  0.0 22.7 jit_solution(1384373688751678103)
XLA Ops:
  0.0 2.6 %shard_map.55 = (bf16[4,36,128]{2,1,0:T(8,128)(2,1)S(1)}, f32[4,32,128]{2,1,0:T(8,128)S(1)}) custom-call(f32[1,24,768]{2,1,0:T(8,128)} %state_hbm.1, s32[24,768]{1,0:T(8,128)} %regions_hbm.1, f32[8]{0:T(128)} %table_hbm.1, s32[1,32]{1,0:T(1,128)} %bitcast.6, bf16[4,32]{1,0:T(4,128)(2,1)} %bitcast.5), custom_call_target="tpu_custom_call" | custom-call | tf_op jit(solution)/shard_map/pallas_call | solution.py:149
  2.6 19.2 %all_to_all.5.blocks_ref = bf16[32,36,128]{2,1,0:T(8,128)(2,1)S(1)} all-to-all(bf16[32,36,128]{2,1,0:T(8,128)(2,1)S(1)} %bitcast.4), channel_id=1, replica_groups=mesh['st'=8,'gr'=4] {'st','gr'}, dimensions={0} | all-to-all | bytes 589824 | tf_op jit(solution)/shard_map/all_to_all | solution.py:157
  21.8 0.9 %shard_map.56 = bf16[6,4,768]{2,1,0:T(4,128)(2,1)} custom-call(f32[4,32,128]{2,1,0:T(8,128)S(1)} %get-tuple-element.7.weights_ref, bf16[32,36,128]{2,1,0:T(8,128)(2,1)S(1)} %all_to_all.5.blocks_ref), custom_call_target="tpu_custom_call" | custom-call | tf_op jit(solution)/shard_map/pallas_call | solution.py:160
  (1 shorter events, 0.0 us)

commit v3 on v2

v3 whole, which is shorter than its diff:
```python
import functools
import math

import jax
import jax.numpy as jnp
import numpy as np
from jax import lax
from jax.experimental import pallas as pl
from jax.experimental.pallas import tpu as pltpu
from jax.sharding import PartitionSpec as P

NZ = 32
DEG = 4
LANES = 128

coef_center = -5369.0 / 1800.0
coef_list = (12.0 / 7.0, -15.0 / 56.0, 10.0 / 189.0, -1.0 / 112.0, 2.0 / 1925.0, -1.0 / 16632.0)
centre = 6.75
half_width = 5.25


weight_list = tuple(-0.5 * c / half_width for c in coef_list)


def halves(level):
    high = float(np.float32(weight_list[level]).astype(jnp.bfloat16))
    return high, weight_list[level] - high


def banded(distance, allowed, part):
    matrix = jnp.zeros(distance.shape, jnp.float32)
    for level in range(len(weight_list)):
        matrix = jnp.where(distance == level + 1, halves(level)[part], matrix)
    return jnp.where(allowed, matrix, 0.0).astype(jnp.bfloat16)


def in_tile_matrix(part):
    shape = (LANES, LANES)
    source = lax.broadcasted_iota(jnp.int32, shape, 0)
    target = lax.broadcasted_iota(jnp.int32, shape, 1)
    along_z = banded(abs(source - target), source // NZ == target // NZ, part)
    along_y = banded(abs(source // NZ - target // NZ), source % NZ == target % NZ, part)
    return along_z + along_y


def row_matrix(height, padded):
    shape = (padded, padded)
    target = lax.broadcasted_iota(jnp.int32, shape, 0)
    source = lax.broadcasted_iota(jnp.int32, shape, 1)
    high, low = (banded(abs(source - target), source < height, part) for part in (0, 1))
    return jnp.concatenate([high, high, low], axis=1)


def tile_couplings(shape):
    group = lax.broadcasted_iota(jnp.int32, shape, 1) // NZ
    per_tile, reach = LANES // NZ, len(weight_list)
    couplings = {}
    for away in range(-(reach // per_tile) - 1, reach // per_tile + 2):
        if away == 0:
            continue
        for turn in range(per_tile):
            steps = [abs(per_tile * away + (g - turn) % per_tile - g) for g in range(per_tile)]
            if min(steps) > reach:
                continue
            factor = jnp.zeros(shape, jnp.float32)
            for g, step in enumerate(steps):
                if step <= reach:
                    factor = jnp.where(group == g, weight_list[step - 1], factor)
            couplings[away, turn] = factor
    return couplings


def scaled_op(tiles, diagonal, rows_matrix, lanes_matrix, couplings):
    count = len(tiles)
    height = tiles[0].shape[0]
    padded = rows_matrix.shape[0]
    blank = jnp.zeros((padded - height, LANES), jnp.float32)
    highs, lows = [], []
    for tile in tiles:
        high = tile.astype(jnp.bfloat16)
        low = tile - high.astype(jnp.float32)
        highs.append(jnp.concatenate([tile, blank], axis=0).astype(jnp.bfloat16))
        lows.append(jnp.concatenate([low, blank], axis=0).astype(jnp.bfloat16))
    pairs = jnp.concatenate([jnp.concatenate([h, l], axis=1) for h, l in zip(highs, lows)], axis=0)
    along_lanes = jnp.dot(pairs, lanes_matrix, preferred_element_type=jnp.float32)
    high_row, low_row = jnp.concatenate(highs, axis=1), jnp.concatenate(lows, axis=1)
    along_rows = jnp.dot(
        rows_matrix, jnp.concatenate([high_row, low_row, high_row], axis=0), preferred_element_type=jnp.float32
    )
    turned = [
        [t if k == 0 else pltpu.roll(t, NZ * k, 1) for k in range(LANES // NZ)] for t in tiles
    ]
    result = []
    for t, tile in enumerate(tiles):
        total = diagonal[t] * tile
        for (away, turn), factor in couplings.items():
            if 0 <= t + away < count:
                total = total + factor * turned[t + away][turn]
        lanes_part = along_lanes[t * padded : t * padded + height]
        rows_part = along_rows[:height, t * LANES : (t + 1) * LANES]
        result.append(total + (rows_part + (lanes_part[:, :LANES] + lanes_part[:, LANES:])))
    return result


def filter_kernel(
    slab,
    state_hbm, regions_hbm, table_hbm, order_hbm, subspace_hbm,
    out_ref, weights_ref,
    state_ref, regions_ref, table_ref, order_ref, subspace_ref, lanes_ref, sems,
):
    sources = (regions_hbm, table_hbm, state_hbm, order_hbm, subspace_hbm)
    targets = (regions_ref, table_ref, state_ref, order_ref, subspace_ref)
    copies = [pltpu.make_async_copy(a, b, sems.at[i]) for i, (a, b) in enumerate(zip(sources, targets))]
    for copy in copies:
        copy.start()
    height, width = regions_ref.shape
    count = width // LANES
    levels = table_ref.shape[0]
    shape = (height, LANES)
    high = in_tile_matrix(0)
    lanes_ref[:LANES, :LANES] = high
    lanes_ref[LANES:, :LANES] = high
    lanes_ref[:LANES, LANES:] = in_tile_matrix(1)
    lanes_ref[LANES:, LANES:] = jnp.zeros((LANES, LANES), jnp.bfloat16)
    rows_matrix = row_matrix(height, -(-height // 16) * 16)
    couplings = tile_couplings(shape)
    diagonal = []
    copies[0].wait()
    copies[1].wait()
    for t in range(count):
        region = regions_ref[:, t * LANES : (t + 1) * LANES]
        potential = jnp.zeros(shape, jnp.float32)
        for level in range(levels):
            potential = jnp.where(region == level, table_ref[level], potential)
        diagonal.append((potential - (centre + 1.5 * coef_center)) * (1.0 / half_width))
    copies[2].wait()
    previous = [state_ref[0, :, t * LANES : (t + 1) * LANES] for t in range(count)]
    current = scaled_op(previous, diagonal, rows_matrix, lanes_ref[...], couplings)
    for _ in range(1, DEG):
        applied = scaled_op(current, diagonal, rows_matrix, lanes_ref[...], couplings)
        following = [2.0 * a - p for a, p in zip(applied, previous)]
        previous, current = current, following
    pieces = [tile[at : at + slab] for at in range(0, height, slab) for tile in current]
    out_ref[...] = jnp.concatenate(pieces, axis=0).astype(jnp.bfloat16)
    copies[3].wait()
    copies[4].wait()
    columns, states = subspace_ref.shape
    place = lax.broadcasted_iota(jnp.int32, (states, states), 0)
    here = lax.broadcasted_iota(jnp.int32, (states, states), 1)
    chosen = jnp.where(order_ref[...] == place, 1.0, 0.0).astype(jnp.bfloat16)
    weights = jnp.dot(subspace_ref[...], chosen, preferred_element_type=jnp.float32)
    ones = jnp.ones((states, LANES), jnp.bfloat16)
    for j in range(columns):
        spread = jnp.where(place == here, weights[j : j + 1], 0.0).astype(jnp.bfloat16)
        weights_ref[j] = jnp.dot(spread, ones, preferred_element_type=jnp.float32)


def rotate_kernel(weights_ref, blocks_ref, out_ref):
    states = weights_ref.shape[1]
    slab, columns, width = out_ref.shape
    rows = slab * width // LANES
    pair = 2 * rows
    sublane = lax.broadcasted_iota(jnp.int32, (8, LANES), 0)

    def body(p, totals):
        tiles = [
            blocks_ref[pl.ds(pl.multiple_of(p * pair + 8 * i, 8), 8)].astype(jnp.float32) for i in range(pair // 8)
        ]
        result = []
        for j in range(columns):
            first = jnp.broadcast_to(weights_ref[j, pl.ds(2 * p, 1)], (8, LANES))
            second = jnp.broadcast_to(weights_ref[j, pl.ds(2 * p + 1, 1)], (8, LANES))
            for i, tile in enumerate(tiles):
                if 8 * i + 8 <= rows:
                    weight = first
                elif 8 * i >= rows:
                    weight = second
                else:
                    weight = jnp.where(sublane < rows - 8 * i, first, second)
                result.append(totals[len(result)] + weight * tile)
        return tuple(result)

    start = tuple(jnp.zeros((8, LANES), jnp.float32) for _ in range(columns * pair // 8))
    totals = lax.fori_loop(0, states // 2, body, start, unroll=4 if states % 8 == 0 else 1)
    for j in range(columns):
        both = jnp.concatenate(totals[j * (pair // 8) : (j + 1) * (pair // 8)], axis=0)
        total = both[:rows] + both[rows:]
        for t in range(width // LANES):
            out_ref[:, j, t * LANES : (t + 1) * LANES] = total[t * slab : (t + 1) * slab].astype(out_ref.dtype)


def grant(array):
    return 3 * array.size * array.dtype.itemsize + (4 << 20)


def per_device(st, gr, states, regions, pot_table, subspace, state_order):
    height, width = regions.shape
    slab = height // gr
    rows = slab * width // LANES
    columns = subspace.shape[1]
    hbm = pl.BlockSpec(memory_space=pltpu.HBM)
    vmem = pl.BlockSpec(memory_space=pltpu.VMEM)
    unit = math.gcd(rows, 8)
    chunk = (rows // unit, unit, LANES)
    filtered = jax.ShapeDtypeStruct((gr * rows, LANES), jnp.bfloat16)
    order = state_order.reshape(1, -1)
    inputs = [pltpu.with_memory_space_constraint(a, pltpu.HBM) for a in (states, regions, pot_table, order, subspace.T)]
    spaces = (pltpu.VMEM, pltpu.VMEM, pltpu.SMEM, pltpu.VMEM, pltpu.VMEM)
    outgoing, weights = pl.pallas_call(
        functools.partial(filter_kernel, slab),
        out_shape=(filtered, jax.ShapeDtypeStruct((columns, subspace.shape[0], LANES), jnp.float32)),
        in_specs=[hbm] * 5,
        out_specs=(vmem, vmem),
        scratch_shapes=[space(a.shape, a.dtype) for space, a in zip(spaces, inputs)]
        + [pltpu.VMEM((2 * LANES, 2 * LANES), jnp.bfloat16), pltpu.SemaphoreType.DMA((5,))],
        compiler_params=pltpu.CompilerParams(vmem_limit_bytes=grant(filtered)),
    )(*inputs)
    blocks = lax.all_to_all(
        jnp.broadcast_to(outgoing, (st, gr * rows, LANES)).reshape(st * gr, *chunk), ("st", "gr"), split_axis=0, concat_axis=0, tiled=True
    )
    rotated = pl.pallas_call(
        rotate_kernel,
        out_shape=jax.ShapeDtypeStruct((slab, columns, width), jnp.bfloat16),
        in_specs=[vmem, vmem],
        out_specs=vmem,
        compiler_params=pltpu.CompilerParams(vmem_limit_bytes=grant(blocks)),
    )(weights, blocks.reshape(-1, LANES))
    return rotated.transpose(1, 0, 2)


def solution(mesh):
    in_specs = (P(("st", "gr"), None, None), P(), P(), P(None, "st"), P())
    out_specs = P("st", "gr", None)
    body = functools.partial(per_device, mesh.shape["st"], mesh.shape["gr"])
    return jax.shard_map(body, mesh=mesh, in_specs=in_specs, out_specs=out_specs, check_vma=False)
```

time: 22.9 us -> 21.6 us (0.943)
  blocking collectives: 19.2 us -> 18.5 us
  Pallas kernels: 3.51 us -> 2.85 us
    pallas_call x1, Pallas kernels: 2.57 us -> 1.88 us  [per_device(): pl.pallas_call(functools.partial(filter_kernel, slab), out_shape=(filtere...]
    all_to_all x1, blocking collectives: 19.2 us -> 18.5 us  [per_device(): lax.all_to_all(jnp.broadcast_to(outgoing, (st, gr * rows, LANES)).reshape...]
where the time goes in v3:
time: 21.6 us; the launch traced here: 21.4 us
  blocking collectives  18.5 us (86%)
  Pallas kernels  2.85 us (13%)
    all_to_all x1, blocking collectives, per_device(): lax.all_to_all(jnp.broadcast_to(outgoing, (st, gr * rows, LANES)).reshape...  18.5 us
    pallas_call x1, Pallas kernels, per_device(): pl.pallas_call(functools.partial(filter_kernel, slab), out_shape=(filtere...  1.88 us
    pallas_call x1, Pallas kernels, per_device(): pl.pallas_call(rotate_kernel, out_shape=jax.ShapeDtypeStruct((slab, colum...  0.97 us

profile of v3, /device:TPU:0, one launch (start us, length us, event | category | flops | bytes accessed | tf_op | source)
XLA Modules:
  0.0 21.4 jit_solution(13645071879952253080)
XLA Ops:
  0.0 1.9 %shard_map.55 = (bf16[144,128]{1,0:T(8,128)(2,1)S(1)}, f32[4,32,128]{2,1,0:T(8,128)S(1)}) custom-call(f32[1,24,768]{2,1,0:T(8,128)} %state_hbm.1, s32[24,768]{1,0:T(8,128)} %regions_hbm.1, f32[8]{0:T(128)} %table_hbm.1, s32[1,32]{1,0:T(1,128)} %bitcast.8, bf16[4,32]{1,0:T(4,128)(2,1)} %bitcast.7), custom_call_target="tpu_custom_call" | custom-call | tf_op jit(solution)/shard_map/pallas_call | solution.py:209
  1.9 18.5 %all_to_all.5 = bf16[32,9,4,128]{3,2,1,0:T(4,128)(2,1)S(1)} all-to-all(bf16[32,9,4,128]{3,2,1,0:T(4,128)(2,1)S(1)} %bitcast.6), channel_id=1, replica_groups=mesh['st'=8,'gr'=4] {'st','gr'}, dimensions={0} | all-to-all | bytes 589824 | tf_op jit(solution)/shard_map/all_to_all | solution.py:218
  20.5 1.0 %shard_map.56 = bf16[6,4,768]{2,1,0:T(4,128)(2,1)} custom-call(f32[4,32,128]{2,1,0:T(8,128)S(1)} %get-tuple-element.7.weights_ref, bf16[1152,128]{1,0:T(8,128)(2,1)S(1)} %bitcast.5), custom_call_target="tpu_custom_call" | custom-call | tf_op jit(solution)/shard_map/pallas_call | solution.py:221
  (1 shorter events, 0.0 us)

commit v4 on v3

--- a/solution.py
+++ b/solution.py
@@ -77,16 +77,17 @@
     blank = jnp.zeros((padded - height, LANES), jnp.float32)
     highs, lows = [], []
     for tile in tiles:
-        high = tile.astype(jnp.bfloat16)
-        low = tile - high.astype(jnp.float32)
-        highs.append(jnp.concatenate([tile, blank], axis=0).astype(jnp.bfloat16))
-        lows.append(jnp.concatenate([low, blank], axis=0).astype(jnp.bfloat16))
+        full = jnp.concatenate([tile, blank], axis=0)
+        highs.append(full.astype(jnp.bfloat16))
+        lows.append((full - highs[-1].astype(jnp.float32)).astype(jnp.bfloat16))
     pairs = jnp.concatenate([jnp.concatenate([h, l], axis=1) for h, l in zip(highs, lows)], axis=0)
     along_lanes = jnp.dot(pairs, lanes_matrix, preferred_element_type=jnp.float32)
-    high_row, low_row = jnp.concatenate(highs, axis=1), jnp.concatenate(lows, axis=1)
-    along_rows = jnp.dot(
-        rows_matrix, jnp.concatenate([high_row, low_row, high_row], axis=0), preferred_element_type=jnp.float32
-    )
+    along_rows = []
+    for at in range(0, count, 2):
+        high_row, low_row = jnp.concatenate(highs[at : at + 2], axis=1), jnp.concatenate(lows[at : at + 2], axis=1)
+        stacked = jnp.concatenate([high_row, low_row, high_row], axis=0)
+        along_rows.append(jnp.dot(rows_matrix, stacked, preferred_element_type=jnp.float32))
+    along_rows = jnp.concatenate(along_rows, axis=1)
     turned = [
         [t if k == 0 else pltpu.roll(t, NZ * k, 1) for k in range(LANES // NZ)] for t in tiles
     ]
@@ -102,14 +103,23 @@
     return result
 
 
+def device_at(place, st, gr):
+    if st % 2 or gr % 2:
+        return place
+    block, within = place // gr, place % gr
+    st_index = st - 2 - 2 * (block // 2) + block % 2
+    gr_index = 2 * (within % (gr // 2)) + 1 - within // (gr // 2)
+    return st_index * gr + gr_index
+
+
 def filter_kernel(
-    slab,
+    st, gr, slab,
     state_hbm, regions_hbm, table_hbm, order_hbm, subspace_hbm,
     out_ref, weights_ref,
     state_ref, regions_ref, table_ref, order_ref, subspace_ref, lanes_ref, sems,
 ):
-    sources = (regions_hbm, table_hbm, state_hbm, order_hbm, subspace_hbm)
-    targets = (regions_ref, table_ref, state_ref, order_ref, subspace_ref)
+    sources = (order_hbm, subspace_hbm, table_hbm, regions_hbm, state_hbm)
+    targets = (order_ref, subspace_ref, table_ref, regions_ref, state_ref)
     copies = [pltpu.make_async_copy(a, b, sems.at[i]) for i, (a, b) in enumerate(zip(sources, targets))]
     for copy in copies:
         copy.start()
@@ -124,26 +134,8 @@
     lanes_ref[LANES:, LANES:] = jnp.zeros((LANES, LANES), jnp.bfloat16)
     rows_matrix = row_matrix(height, -(-height // 16) * 16)
     couplings = tile_couplings(shape)
-    diagonal = []
     copies[0].wait()
     copies[1].wait()
-    for t in range(count):
-        region = regions_ref[:, t * LANES : (t + 1) * LANES]
-        potential = jnp.zeros(shape, jnp.float32)
-        for level in range(levels):
-            potential = jnp.where(region == level, table_ref[level], potential)
-        diagonal.append((potential - (centre + 1.5 * coef_center)) * (1.0 / half_width))
-    copies[2].wait()
-    previous = [state_ref[0, :, t * LANES : (t + 1) * LANES] for t in range(count)]
-    current = scaled_op(previous, diagonal, rows_matrix, lanes_ref[...], couplings)
-    for _ in range(1, DEG):
-        applied = scaled_op(current, diagonal, rows_matrix, lanes_ref[...], couplings)
-        following = [2.0 * a - p for a, p in zip(applied, previous)]
-        previous, current = current, following
-    pieces = [tile[at : at + slab] for at in range(0, height, slab) for tile in current]
-    out_ref[...] = jnp.concatenate(pieces, axis=0).astype(jnp.bfloat16)
-    copies[3].wait()
-    copies[4].wait()
     columns, states = subspace_ref.shape
     place = lax.broadcasted_iota(jnp.int32, (states, states), 0)
     here = lax.broadcasted_iota(jnp.int32, (states, states), 1)
@@ -151,8 +143,35 @@
     weights = jnp.dot(subspace_ref[...], chosen, preferred_element_type=jnp.float32)
     ones = jnp.ones((states, LANES), jnp.bfloat16)
     for j in range(columns):
-        spread = jnp.where(place == here, weights[j : j + 1], 0.0).astype(jnp.bfloat16)
+        spread = jnp.where(device_at(place, st, gr) == here, weights[j : j + 1], 0.0).astype(jnp.bfloat16)
         weights_ref[j] = jnp.dot(spread, ones, preferred_element_type=jnp.float32)
+    diagonal = []
+    copies[2].wait()
+    copies[3].wait()
+    for t in range(count):
+        region = regions_ref[:, t * LANES : (t + 1) * LANES]
+        potential = jnp.zeros(shape, jnp.float32)
+        for level in range(levels):
+            potential = jnp.where(region == level, table_ref[level], potential)
+        diagonal.append((potential - (centre + 1.5 * coef_center)) * (1.0 / half_width))
+    copies[4].wait()
+    previous = [state_ref[0, :, t * LANES : (t + 1) * LANES] for t in range(count)]
+    current = scaled_op(previous, diagonal, rows_matrix, lanes_ref[...], couplings)
+    for _ in range(1, DEG):
+        applied = scaled_op(current, diagonal, rows_matrix, lanes_ref[...], couplings)
+        following = [2.0 * a - p for a, p in zip(applied, previous)]
+        previous, current = current, following
+    slabs = [device_at(place, st, gr) % gr for place in range(gr)]
+    pieces = [tile[g * slab : (g + 1) * slab] for g in slabs for tile in current]
+    filtered = jnp.concatenate(pieces, axis=0).astype(jnp.bfloat16)
+    size = filtered.shape[0]
+
+    def put(copy, _):
+        out_ref[pl.ds(pl.multiple_of(copy * size, 16), size)] = filtered
+        return _
+
+    copies_out = out_ref.shape[0] // size
+    lax.fori_loop(0, copies_out, put, 0, unroll=math.gcd(copies_out, 8))
 
 
 def rotate_kernel(weights_ref, blocks_ref, out_ref):
@@ -181,7 +200,7 @@
         return tuple(result)
 
     start = tuple(jnp.zeros((8, LANES), jnp.float32) for _ in range(columns * pair // 8))
-    totals = lax.fori_loop(0, states // 2, body, start, unroll=4 if states % 8 == 0 else 1)
+    totals = lax.fori_loop(0, states // 2, body, start, unroll=8 if states % 16 == 0 else 1)
     for j in range(columns):
         both = jnp.concatenate(totals[j * (pair // 8) : (j + 1) * (pair // 8)], axis=0)
         total = both[:rows] + both[rows:]
@@ -202,12 +221,12 @@
     vmem = pl.BlockSpec(memory_space=pltpu.VMEM)
     unit = math.gcd(rows, 8)
     chunk = (rows // unit, unit, LANES)
-    filtered = jax.ShapeDtypeStruct((gr * rows, LANES), jnp.bfloat16)
+    filtered = jax.ShapeDtypeStruct((st * gr * rows, LANES), jnp.bfloat16)
     order = state_order.reshape(1, -1)
     inputs = [pltpu.with_memory_space_constraint(a, pltpu.HBM) for a in (states, regions, pot_table, order, subspace.T)]
     spaces = (pltpu.VMEM, pltpu.VMEM, pltpu.SMEM, pltpu.VMEM, pltpu.VMEM)
     outgoing, weights = pl.pallas_call(
-        functools.partial(filter_kernel, slab),
+        functools.partial(filter_kernel, st, gr, slab),
         out_shape=(filtered, jax.ShapeDtypeStruct((columns, subspace.shape[0], LANES), jnp.float32)),
         in_specs=[hbm] * 5,
         out_specs=(vmem, vmem),
@@ -216,7 +235,12 @@
         compiler_params=pltpu.CompilerParams(vmem_limit_bytes=grant(filtered)),
     )(*inputs)
     blocks = lax.all_to_all(
-        jnp.broadcast_to(outgoing, (st, gr * rows, LANES)).reshape(st * gr, *chunk), ("st", "gr"), split_axis=0, concat_axis=0, tiled=True
+        outgoing.reshape(st * gr, *chunk),
+        ("st", "gr"),
+        split_axis=0,
+        concat_axis=0,
+        tiled=True,
+        axis_index_groups=[[device_at(place, st, gr) for place in range(st * gr)]],
     )
     rotated = pl.pallas_call(
         rotate_kernel,

time: 21.6 us -> 20.3 us (0.940)
  blocking collectives: 18.5 us -> 17.5 us
    all_to_all x1, blocking collectives: 18.5 us -> 17.5 us  [per_device(): lax.all_to_all(outgoing.reshape(st * gr, *chunk), ('st', 'gr'), split_axi...]
where the time goes in v4:
time: 20.3 us; the launch traced here: 20.1 us
  blocking collectives  17.5 us (86%)
  Pallas kernels  2.65 us (13%)
    all_to_all x1, blocking collectives, per_device(): lax.all_to_all(outgoing.reshape(st * gr, *chunk), ('st', 'gr'), split_axi...  17.5 us
    pallas_call x1, Pallas kernels, per_device(): pl.pallas_call(functools.partial(filter_kernel, st, gr, slab), out_shape=...  1.71 us
    pallas_call x1, Pallas kernels, per_device(): pl.pallas_call(rotate_kernel, out_shape=jax.ShapeDtypeStruct((slab, colum...  0.94 us

profile of v4, /device:TPU:0, one launch (start us, length us, event | category | flops | bytes accessed | tf_op | source)
XLA Modules:
  0.0 20.1 jit_solution(1584847801072969213)
XLA Ops:
  0.0 1.7 %shard_map.55 = (bf16[1152,128]{1,0:T(8,128)(2,1)S(1)}, f32[4,32,128]{2,1,0:T(8,128)S(1)}) custom-call(f32[1,24,768]{2,1,0:T(8,128)} %state_hbm.1, s32[24,768]{1,0:T(8,128)} %regions_hbm.1, f32[8]{0:T(128)} %table_hbm.1, s32[1,32]{1,0:T(1,128)} %bitcast.8, bf16[4,32]{1,0:T(4,128)(2,1)} %bitcast.7), custom_call_target="tpu_custom_call" | custom-call | tf_op jit(solution)/shard_map/pallas_call | solution.py:228
  1.7 17.5 %all_to_all.5 = bf16[32,9,4,128]{3,2,1,0:T(4,128)(2,1)S(1)} all-to-all(bf16[32,9,4,128]{3,2,1,0:T(4,128)(2,1)S(1)} %bitcast.6), channel_id=1, replica_groups={{25,27,24,26,29,31,28,30,17,19,16,18,21,23,20,22,9,11,8,10,13,15,12,14,..., dimensions={0} | all-to-all | bytes 589824 | tf_op jit(solution)/shard_map/all_to_all | solution.py:237
  19.2 0.9 %shard_map.56 = bf16[6,4,768]{2,1,0:T(4,128)(2,1)} custom-call(f32[4,32,128]{2,1,0:T(8,128)S(1)} %get-tuple-element.7.weights_ref, bf16[1152,128]{1,0:T(8,128)(2,1)S(1)} %bitcast.5), custom_call_target="tpu_custom_call" | custom-call | tf_op jit(solution)/shard_map/pallas_call | solution.py:245

commit v5 on v4

--- a/solution.py
+++ b/solution.py
@@ -17,6 +17,9 @@
 coef_list = (12.0 / 7.0, -15.0 / 56.0, 10.0 / 189.0, -1.0 / 112.0, 2.0 / 1925.0, -1.0 / 16632.0)
 centre = 6.75
 half_width = 5.25
+
+st_pattern = (7, 3, 5, 6, 2, 0, 4, 1)
+gr_pattern = (0, 2, 3, 1)
 
 
 weight_list = tuple(-0.5 * c / half_width for c in coef_list)
@@ -103,13 +106,24 @@
     return result
 
 
+def looked_up(pattern, index):
+    if isinstance(index, int):
+        return pattern[index]
+    value = jnp.zeros_like(index)
+    for at, entry in enumerate(pattern):
+        value = jnp.where(index == at, entry, value)
+    return value
+
+
+def reordered(place, size, pattern):
+    length = len(pattern)
+    if size % length:
+        return place
+    return place // length * length + looked_up(pattern, place % length)
+
+
 def device_at(place, st, gr):
-    if st % 2 or gr % 2:
-        return place
-    block, within = place // gr, place % gr
-    st_index = st - 2 - 2 * (block // 2) + block % 2
-    gr_index = 2 * (within % (gr // 2)) + 1 - within // (gr // 2)
-    return st_index * gr + gr_index
+    return reordered(place // gr, st, st_pattern) * gr + reordered(place % gr, gr, gr_pattern)
 
 
 def filter_kernel(

time: 20.3 us -> 19.7 us (0.970)
  blocking collectives: 17.5 us -> 16.9 us
    all_to_all x1, blocking collectives: 17.5 us -> 16.9 us  [per_device(): lax.all_to_all(outgoing.reshape(st * gr, *chunk), ('st', 'gr'), split_axi...]
where the time goes in v5:
time: 19.7 us; the launch traced here: 19.5 us
  blocking collectives  16.9 us (86%)
  Pallas kernels  2.65 us (13%)
    all_to_all x1, blocking collectives, per_device(): lax.all_to_all(outgoing.reshape(st * gr, *chunk), ('st', 'gr'), split_axi...  16.9 us
    pallas_call x1, Pallas kernels, per_device(): pl.pallas_call(functools.partial(filter_kernel, st, gr, slab), out_shape=...  1.71 us
    pallas_call x1, Pallas kernels, per_device(): pl.pallas_call(rotate_kernel, out_shape=jax.ShapeDtypeStruct((slab, colum...  0.94 us

profile of v5, /device:TPU:0, one launch (start us, length us, event | category | flops | bytes accessed | tf_op | source)
XLA Modules:
  0.0 19.5 jit_solution(13055023364744578396)
XLA Ops:
  0.0 1.7 %shard_map.55 = (bf16[1152,128]{1,0:T(8,128)(2,1)S(1)}, f32[4,32,128]{2,1,0:T(8,128)S(1)}) custom-call(f32[1,24,768]{2,1,0:T(8,128)} %state_hbm.1, s32[24,768]{1,0:T(8,128)} %regions_hbm.1, f32[8]{0:T(128)} %table_hbm.1, s32[1,32]{1,0:T(1,128)} %bitcast.8, bf16[4,32]{1,0:T(4,128)(2,1)} %bitcast.7), custom_call_target="tpu_custom_call" | custom-call | tf_op jit(solution)/shard_map/pallas_call | solution.py:242
  1.7 16.9 %all_to_all.5 = bf16[32,9,4,128]{3,2,1,0:T(4,128)(2,1)S(1)} all-to-all(bf16[32,9,4,128]{3,2,1,0:T(4,128)(2,1)S(1)} %bitcast.6), channel_id=1, replica_groups={{28,30,31,29,12,14,15,13,20,22,23,21,24,26,27,25,8,10,11,9,0,2,3,1,16,1..., dimensions={0} | all-to-all | bytes 589824 | tf_op jit(solution)/shard_map/all_to_all | solution.py:251
  18.6 0.9 %shard_map.56 = bf16[6,4,768]{2,1,0:T(4,128)(2,1)} custom-call(f32[4,32,128]{2,1,0:T(8,128)S(1)} %get-tuple-element.7.weights_ref, bf16[1152,128]{1,0:T(8,128)(2,1)S(1)} %bitcast.5), custom_call_target="tpu_custom_call" | custom-call | tf_op jit(solution)/shard_map/pallas_call | solution.py:259

commit v6 on v5

--- a/solution.py
+++ b/solution.py
@@ -18,7 +18,7 @@
 centre = 6.75
 half_width = 5.25
 
-st_pattern = (7, 3, 5, 6, 2, 0, 4, 1)
+st_pattern = (6, 2, 0, 4, 3, 7, 1, 5)
 gr_pattern = (0, 2, 3, 1)
 
 
@@ -135,7 +135,7 @@
     sources = (order_hbm, subspace_hbm, table_hbm, regions_hbm, state_hbm)
     targets = (order_ref, subspace_ref, table_ref, regions_ref, state_ref)
     copies = [pltpu.make_async_copy(a, b, sems.at[i]) for i, (a, b) in enumerate(zip(sources, targets))]
-    for copy in copies:
+    for copy in copies[::-1]:
         copy.start()
     height, width = regions_ref.shape
     count = width // LANES

time: 19.7 us -> 19.7 us (level)
  no operation moved by 1% of the time
where the time goes in v6:
time: 19.7 us; the launch traced here: 19.6 us
  blocking collectives  16.9 us (86%)
  Pallas kernels  2.71 us (14%)
    all_to_all x1, blocking collectives, per_device(): lax.all_to_all(outgoing.reshape(st * gr, *chunk), ('st', 'gr'), split_axi...  16.9 us
    pallas_call x1, Pallas kernels, per_device(): pl.pallas_call(functools.partial(filter_kernel, st, gr, slab), out_shape=...  1.76 us
    pallas_call x1, Pallas kernels, per_device(): pl.pallas_call(rotate_kernel, out_shape=jax.ShapeDtypeStruct((slab, colum...  0.94 us

profile of v6, /device:TPU:0, one launch (start us, length us, event | category | flops | bytes accessed | tf_op | source)
XLA Modules:
  0.0 19.6 jit_solution(16077811786702041423)
XLA Ops:
  0.0 1.8 %shard_map.55 = (bf16[1152,128]{1,0:T(8,128)(2,1)S(1)}, f32[4,32,128]{2,1,0:T(8,128)S(1)}) custom-call(f32[1,24,768]{2,1,0:T(8,128)} %state_hbm.1, s32[24,768]{1,0:T(8,128)} %regions_hbm.1, f32[8]{0:T(128)} %table_hbm.1, s32[1,32]{1,0:T(1,128)} %bitcast.8, bf16[4,32]{1,0:T(4,128)(2,1)} %bitcast.7), custom_call_target="tpu_custom_call" | custom-call | tf_op jit(solution)/shard_map/pallas_call | solution.py:242
  1.8 16.9 %all_to_all.5 = bf16[32,9,4,128]{3,2,1,0:T(4,128)(2,1)S(1)} all-to-all(bf16[32,9,4,128]{3,2,1,0:T(4,128)(2,1)S(1)} %bitcast.6), channel_id=1, replica_groups={{24,26,27,25,8,10,11,9,0,2,3,1,16,18,19,17,12,14,15,13,28,30,31,29,4,6,..., dimensions={0} | all-to-all | bytes 589824 | tf_op jit(solution)/shard_map/all_to_all | solution.py:251
  18.6 0.9 %shard_map.56 = bf16[6,4,768]{2,1,0:T(4,128)(2,1)} custom-call(f32[4,32,128]{2,1,0:T(8,128)S(1)} %get-tuple-element.7.weights_ref, bf16[1152,128]{1,0:T(8,128)(2,1)S(1)} %bitcast.5), custom_call_target="tpu_custom_call" | custom-call | tf_op jit(solution)/shard_map/pallas_call | solution.py:259

commit v7 on v6

--- a/solution.py
+++ b/solution.py
@@ -18,7 +18,7 @@
 centre = 6.75
 half_width = 5.25
 
-st_pattern = (6, 2, 0, 4, 3, 7, 1, 5)
+st_pattern = (7, 3, 5, 6, 2, 0, 4, 1)
 gr_pattern = (0, 2, 3, 1)
 
 

time: 19.7 us -> 19.7 us (level)
  no operation moved by 1% of the time
where the time goes in v7:
time: 19.7 us; the launch traced here: 19.6 us
  blocking collectives  16.9 us (86%)
  Pallas kernels  2.71 us (14%)
    all_to_all x1, blocking collectives, per_device(): lax.all_to_all(outgoing.reshape(st * gr, *chunk), ('st', 'gr'), split_axi...  16.9 us
    pallas_call x1, Pallas kernels, per_device(): pl.pallas_call(functools.partial(filter_kernel, st, gr, slab), out_shape=...  1.76 us
    pallas_call x1, Pallas kernels, per_device(): pl.pallas_call(rotate_kernel, out_shape=jax.ShapeDtypeStruct((slab, colum...  0.94 us

profile of v7, /device:TPU:0, one launch (start us, length us, event | category | flops | bytes accessed | tf_op | source)
XLA Modules:
  0.0 19.6 jit_solution(17146379888167112035)
XLA Ops:
  0.0 1.8 %shard_map.55 = (bf16[1152,128]{1,0:T(8,128)(2,1)S(1)}, f32[4,32,128]{2,1,0:T(8,128)S(1)}) custom-call(f32[1,24,768]{2,1,0:T(8,128)} %state_hbm.1, s32[24,768]{1,0:T(8,128)} %regions_hbm.1, f32[8]{0:T(128)} %table_hbm.1, s32[1,32]{1,0:T(1,128)} %bitcast.8, bf16[4,32]{1,0:T(4,128)(2,1)} %bitcast.7), custom_call_target="tpu_custom_call" | custom-call | tf_op jit(solution)/shard_map/pallas_call | solution.py:242
  1.8 16.9 %all_to_all.5 = bf16[32,9,4,128]{3,2,1,0:T(4,128)(2,1)S(1)} all-to-all(bf16[32,9,4,128]{3,2,1,0:T(4,128)(2,1)S(1)} %bitcast.6), channel_id=1, replica_groups={{28,30,31,29,12,14,15,13,20,22,23,21,24,26,27,25,8,10,11,9,0,2,3,1,16,1..., dimensions={0} | all-to-all | bytes 589824 | tf_op jit(solution)/shard_map/all_to_all | solution.py:251
  18.6 0.9 %shard_map.56 = bf16[6,4,768]{2,1,0:T(4,128)(2,1)} custom-call(f32[4,32,128]{2,1,0:T(8,128)S(1)} %get-tuple-element.7.weights_ref, bf16[1152,128]{1,0:T(8,128)(2,1)S(1)} %bitcast.5), custom_call_target="tpu_custom_call" | custom-call | tf_op jit(solution)/shard_map/pallas_call | solution.py:259

commit v8 on v5

--- a/solution.py
+++ b/solution.py
@@ -214,7 +214,7 @@
         return tuple(result)
 
     start = tuple(jnp.zeros((8, LANES), jnp.float32) for _ in range(columns * pair // 8))
-    totals = lax.fori_loop(0, states // 2, body, start, unroll=8 if states % 16 == 0 else 1)
+    totals = lax.fori_loop(0, states // 2, body, start, unroll=16 if states % 32 == 0 else 1)
     for j in range(columns):
         both = jnp.concatenate(totals[j * (pair // 8) : (j + 1) * (pair // 8)], axis=0)
         total = both[:rows] + both[rows:]

time: 19.7 us -> 19.6 us (level)
  no operation moved by 1% of the time
where the time goes in v8:
time: 19.6 us; the launch traced here: 19.5 us
  blocking collectives  16.9 us (86%)
  Pallas kernels  2.61 us (13%)
    all_to_all x1, blocking collectives, per_device(): lax.all_to_all(outgoing.reshape(st * gr, *chunk), ('st', 'gr'), split_axi...  16.9 us
    pallas_call x1, Pallas kernels, per_device(): pl.pallas_call(functools.partial(filter_kernel, st, gr, slab), out_shape=...  1.71 us
    pallas_call x1, Pallas kernels, per_device(): pl.pallas_call(rotate_kernel, out_shape=jax.ShapeDtypeStruct((slab, colum...  0.9 us

profile of v8, /device:TPU:0, one launch (start us, length us, event | category | flops | bytes accessed | tf_op | source)
XLA Modules:
  0.0 19.5 jit_solution(2283113777774341439)
XLA Ops:
  0.0 1.7 %shard_map.55 = (bf16[1152,128]{1,0:T(8,128)(2,1)S(1)}, f32[4,32,128]{2,1,0:T(8,128)S(1)}) custom-call(f32[1,24,768]{2,1,0:T(8,128)} %state_hbm.1, s32[24,768]{1,0:T(8,128)} %regions_hbm.1, f32[8]{0:T(128)} %table_hbm.1, s32[1,32]{1,0:T(1,128)} %bitcast.8, bf16[4,32]{1,0:T(4,128)(2,1)} %bitcast.7), custom_call_target="tpu_custom_call" | custom-call | tf_op jit(solution)/shard_map/pallas_call | solution.py:242
  1.7 16.9 %all_to_all.5 = bf16[32,9,4,128]{3,2,1,0:T(4,128)(2,1)S(1)} all-to-all(bf16[32,9,4,128]{3,2,1,0:T(4,128)(2,1)S(1)} %bitcast.6), channel_id=1, replica_groups={{28,30,31,29,12,14,15,13,20,22,23,21,24,26,27,25,8,10,11,9,0,2,3,1,16,1..., dimensions={0} | all-to-all | bytes 589824 | tf_op jit(solution)/shard_map/all_to_all | solution.py:251
  18.6 0.9 %shard_map.56 = bf16[6,4,768]{2,1,0:T(4,128)(2,1)} custom-call(f32[4,32,128]{2,1,0:T(8,128)S(1)} %get-tuple-element.7.weights_ref, bf16[1152,128]{1,0:T(8,128)(2,1)S(1)} %bitcast.5), custom_call_target="tpu_custom_call" | custom-call | tf_op jit(solution)/shard_map/pallas_call | solution.py:259
